TPU v7x, 32 devices: a whole 2x2x4 slice. The times are simulated.
32 devices in a mesh: group: 2 (over y), replica: 4 (over z), seq: 4 (over x, core).
Axes of the slice: x: 2, y: 2, z: 4, core: 2. Of those that a mesh axis runs over, the one named last changes fastest.
Arguments:
- features: bfloat16 [16, 2048, 1152], P(('group', 'replica'), 'seq'), may hold values from -6 to 6
- condition: bfloat16 [16, 1152], P(('group', 'replica')), may hold values from -6 to 6
- modulator: bfloat16 [1152, 6912], P('group'), may hold values from -0.1875 to 0.1875
- modulator_bias: bfloat16 [6912], P('group'), may hold values from -3 to 3
- projector: bfloat16 [1152, 3456], P('group'), may hold values from -0.1875 to 0.1875
- projector_bias: bfloat16 [2304], P('group'), may hold values from -0.29882812 to 0.29882812
- combiner: bfloat16 [1152, 1152], P('group'), may hold values from -3 to 3
- combiner_bias: bfloat16 [1152], P('group'), may hold values from -3 to 3
- expander: bfloat16 [1152, 4608], P('group'), may hold values from -0.1875 to 0.1875
- expander_bias: bfloat16 [4608], P('group'), may hold values from -3 to 3
- reducer: bfloat16 [4608, 1152], P('group'), may hold values from -0.09375 to 0.09375
- reducer_bias: bfloat16 [1152], P('group'), may hold values from -3 to 3
- cotangent: bfloat16 [16, 2048, 1152], P(('group', 'replica'), 'seq'), may hold values from -6 to 6
Outputs:
- block_output: bfloat16 [16, 2048, 1152], P(('group', 'replica'), 'seq')
- features_grad: float32 [16, 2048, 1152], P(('group', 'replica'), 'seq')
- condition_grad: float32 [16, 1152], P(('group', 'replica'))
- modulator_grad: float32 [1152, 6912], P('group')
- modulator_bias_grad: float32 [6912], P('group')
- projector_grad: float32 [1152, 3456], P('group')
- projector_bias_grad: float32 [2304], P('group')
- combiner_grad: float32 [1152, 1152], P('group')
- combiner_bias_grad: float32 [1152], P('group')
- expander_grad: float32 [1152, 4608], P('group')
- expander_bias_grad: float32 [4608], P('group')
- reducer_grad: float32 [4608, 1152], P('group')
- reducer_bias_grad: float32 [1152], P('group')
All inputs are finite; a program needn't handle non-finite values.
Results may differ from a plain program's by a relative error of at most 0.018.
Values may be sent and summed in bfloat16 or wider, within the bound.
No kernel may reach another device: no remote copies, remote signals or barrier semaphores. Data moves between devices by JAX's collectives and lax.ppermute only.
A program may use at most 448 MiB of HBM per device.

v0:
```python
from functools import partial
import jax
import jax.numpy as jnp
from jax import lax
from jax.sharding import PartitionSpec as P

HEADS = 16
HEAD_DIM = 72
HEAD_SET = 4


def normalize(values):
    centre = jnp.mean(values, -1, keepdims=True)
    centred = values - centre
    inverse = lax.rsqrt(jnp.mean(centred * centred, -1, keepdims=True) + 1e-06)
    return (centred * inverse, inverse)


def normalize_back(grad_in, normed, inverse):
    return (
        grad_in
        - jnp.mean(grad_in, -1, keepdims=True)
        - normed * jnp.mean(grad_in * normed, -1, keepdims=True)
    ) * inverse


def matmul(operand, matrix):
    return jnp.einsum("btd,de->bte", operand, matrix, preferred_element_type=jnp.float32)


def matmul_back(operand, matrix):
    return jnp.einsum("bte,de->btd", operand, matrix, preferred_element_type=jnp.float32)


def outer_sum(operand, other):
    return jnp.einsum("btd,bte->de", operand, other, preferred_element_type=jnp.float32)


def split_heads(tensor):
    return tensor.reshape(tensor.shape[0], tensor.shape[1], HEADS, HEAD_DIM)


def to_sets(tensor):
    return tensor.reshape(tensor.shape[0], -1, HEAD_SET, tensor.shape[-1]).transpose(1, 0, 2, 3)


def from_sets(tensor):
    return tensor.transpose(1, 0, 2, 3).reshape(
        tensor.shape[1], tensor.shape[0] * tensor.shape[2] * tensor.shape[3]
    )


def attend_set(packed):
    query_block, key_block, value_block = packed
    scaling = HEAD_DIM ** (-0.5)
    scores = (
        jnp.einsum("qhd,khd->hqk", query_block, key_block, preferred_element_type=jnp.float32)
        * scaling
    )
    row_max = jnp.max(scores, -1, keepdims=True)
    exponent = jnp.exp(scores - row_max)
    row_total = jnp.sum(exponent, -1, keepdims=True)
    probabilities = (exponent / row_total).astype(jnp.bfloat16)
    context = jnp.einsum(
        "hqk,khd->qhd", probabilities, value_block, preferred_element_type=jnp.float32
    )
    log_total = (row_max + jnp.log(row_total))[..., 0]
    return (context, log_total)


def attend(packed):
    query_block, key_block, value_block = packed
    context_sets, total_sets = lax.map(
        attend_set, (to_sets(query_block), to_sets(key_block), to_sets(value_block))
    )
    return (from_sets(context_sets), total_sets.reshape(HEADS, -1))


def attend_back_set(packed):
    query_block, key_block, value_block, context_block, log_total = packed
    scaling = HEAD_DIM ** (-0.5)
    scores = (
        jnp.einsum("qhd,khd->hqk", query_block, key_block, preferred_element_type=jnp.float32)
        * scaling
    )
    probabilities = jnp.exp(scores - log_total[..., None])
    probs_grad = jnp.einsum(
        "qhd,khd->hqk", context_block, value_block, preferred_element_type=jnp.float32
    )
    row_dot = jnp.sum(probabilities * probs_grad, -1, keepdims=True)
    scores_grad = (probabilities * (probs_grad - row_dot)).astype(jnp.bfloat16)
    query_grad = (
        jnp.einsum("hqk,khd->qhd", scores_grad, key_block, preferred_element_type=jnp.float32)
        * scaling
    )
    key_part = (
        jnp.einsum("hqk,qhd->khd", scores_grad, query_block, preferred_element_type=jnp.float32)
        * scaling
    )
    value_part = jnp.einsum(
        "hqk,qhd->khd",
        probabilities.astype(jnp.bfloat16),
        context_block,
        preferred_element_type=jnp.float32,
    )
    return (query_grad, key_part, value_part)


def attend_back(packed):
    query_block, key_block, value_block, context_block, log_total = packed
    total_sets = log_total.reshape(-1, HEAD_SET, log_total.shape[-1])
    query_sets, key_sets, value_sets = lax.map(
        attend_back_set,
        (
            to_sets(query_block),
            to_sets(key_block),
            to_sets(value_block),
            to_sets(context_block),
            total_sets,
        ),
    )
    return (from_sets(query_sets), from_sets(key_sets), from_sets(value_sets))


def body(
    features,
    condition,
    modulator,
    modulator_bias,
    projector,
    projector_bias,
    combiner,
    combiner_bias,
    expander,
    expander_bias,
    reducer,
    reducer_bias,
    cotangent,
):
    shards = (
        modulator,
        modulator_bias,
        projector,
        projector_bias,
        combiner,
        combiner_bias,
        expander,
        expander_bias,
        reducer,
        reducer_bias,
    )
    gathered = (
        lax.all_gather(shards[0], "group", axis=0, tiled=True),
        lax.all_gather(shards[1], "group", axis=0, tiled=True),
        lax.all_gather(shards[2], "group", axis=0, tiled=True),
        lax.all_gather(shards[3], "group", axis=0, tiled=True),
        lax.all_gather(shards[4], "group", axis=0, tiled=True),
        lax.all_gather(shards[5], "group", axis=0, tiled=True),
        lax.all_gather(shards[6], "group", axis=0, tiled=True),
        lax.all_gather(shards[7], "group", axis=0, tiled=True),
        lax.all_gather(shards[8], "group", axis=0, tiled=True),
        lax.all_gather(shards[9], "group", axis=0, tiled=True),
    )
    (
        full_modulator,
        full_mod_bias,
        full_projector,
        full_proj_bias,
        full_combiner,
        full_comb_bias,
        full_expander,
        full_exp_bias,
        full_reducer,
        full_red_bias,
    ) = gathered
    model_width = features.shape[-1]
    cond_float = condition.astype(jnp.float32)
    silu_low = jax.nn.silu(cond_float).astype(jnp.bfloat16)
    modulation = jnp.dot(
        silu_low, full_modulator, preferred_element_type=jnp.float32
    ) + full_mod_bias.astype(jnp.float32)
    pieces = [
        modulation[:, None, position * model_width : (position + 1) * model_width]
        for position in range(6)
    ]
    shift_attn, scale_attn, gate_attn, shift_mlp, scale_mlp, gate_mlp = pieces
    residual = features.astype(jnp.float32)
    normed_one, inverse_one = normalize(residual)
    attn_in = (normed_one * (1.0 + scale_attn) + shift_attn).astype(jnp.bfloat16)
    bias_float = full_proj_bias.astype(jnp.float32)
    qkv_bias = jnp.concatenate(
        [bias_float[:model_width], jnp.zeros((model_width,), jnp.float32), bias_float[model_width:]]
    )
    qkv_low = (matmul(attn_in, full_projector) + qkv_bias).astype(jnp.bfloat16)
    queries = qkv_low[..., :model_width]
    keys_own = qkv_low[..., model_width : 2 * model_width]
    values_own = qkv_low[..., 2 * model_width :]
    keys_all, values_all = (
        lax.all_gather(keys_own, "seq", axis=1, tiled=True),
        lax.all_gather(values_own, "seq", axis=1, tiled=True),
    )
    context, log_total = lax.map(
        attend, (split_heads(queries), split_heads(keys_all), split_heads(values_all))
    )
    context_low = context.astype(jnp.bfloat16)
    attn_out = matmul(context_low, full_combiner) + full_comb_bias.astype(jnp.float32)
    hidden = residual + gate_attn * attn_out
    normed_two, inverse_two = normalize(hidden)
    mlp_in = (normed_two * (1.0 + scale_mlp) + shift_mlp).astype(jnp.bfloat16)
    expanded = matmul(mlp_in, full_expander) + full_exp_bias.astype(jnp.float32)
    activated = jax.nn.gelu(expanded, approximate=True).astype(jnp.bfloat16)
    reduced = matmul(activated, full_reducer) + full_red_bias.astype(jnp.float32)
    block_output = (hidden + gate_mlp * reduced).astype(jnp.bfloat16)
    regathered = (
        lax.all_gather(shards[0], "group", axis=0, tiled=True),
        lax.all_gather(shards[1], "group", axis=0, tiled=True),
        lax.all_gather(shards[2], "group", axis=0, tiled=True),
        lax.all_gather(shards[3], "group", axis=0, tiled=True),
        lax.all_gather(shards[4], "group", axis=0, tiled=True),
        lax.all_gather(shards[5], "group", axis=0, tiled=True),
        lax.all_gather(shards[6], "group", axis=0, tiled=True),
        lax.all_gather(shards[7], "group", axis=0, tiled=True),
        lax.all_gather(shards[8], "group", axis=0, tiled=True),
        lax.all_gather(shards[9], "group", axis=0, tiled=True),
    )
    back_modulator = regathered[0]
    back_projector = regathered[2]
    back_combiner = regathered[4]
    back_expander = regathered[6]
    back_reducer = regathered[8]
    upstream = cotangent.astype(jnp.float32)
    reduced_grad = (gate_mlp * upstream).astype(jnp.bfloat16)
    gate_mlp_grad = jnp.sum(upstream * reduced, 1)
    reducer_grad = outer_sum(activated, reduced_grad)
    reducer_bias_grad = jnp.sum(reduced_grad.astype(jnp.float32), (0, 1))
    activated_grad = matmul_back(reduced_grad, back_reducer)
    unused_value, gelu_back = jax.vjp(partial(jax.nn.gelu, approximate=True), expanded)
    expanded_grad = gelu_back(activated_grad)[0].astype(jnp.bfloat16)
    expander_grad = outer_sum(mlp_in, expanded_grad)
    expander_bias_grad = jnp.sum(expanded_grad.astype(jnp.float32), (0, 1))
    mlp_in_grad = matmul_back(expanded_grad, back_expander)
    scale_mlp_grad = jnp.sum(mlp_in_grad * normed_two, 1)
    shift_mlp_grad = jnp.sum(mlp_in_grad, 1)
    hidden_grad = upstream + normalize_back(
        mlp_in_grad * (1.0 + scale_mlp), normed_two, inverse_two
    )
    attn_out_grad = (gate_attn * hidden_grad).astype(jnp.bfloat16)
    gate_attn_grad = jnp.sum(hidden_grad * attn_out, 1)
    combiner_grad = outer_sum(context_low, attn_out_grad)
    combiner_bias_grad = jnp.sum(attn_out_grad.astype(jnp.float32), (0, 1))
    context_grad = matmul_back(attn_out_grad, back_combiner).astype(jnp.bfloat16)
    keys_back, values_back = (
        lax.all_gather(keys_own, "seq", axis=1, tiled=True),
        lax.all_gather(values_own, "seq", axis=1, tiled=True),
    )
    query_grad, key_part, value_part = lax.map(
        attend_back,
        (
            split_heads(queries),
            split_heads(keys_back),
            split_heads(values_back),
            split_heads(context_grad),
            log_total,
        ),
    )
    key_grad, value_grad = (
        lax.psum_scatter(key_part, "seq", scatter_dimension=1, tiled=True),
        lax.psum_scatter(value_part, "seq", scatter_dimension=1, tiled=True),
    )
    qkv_grad = jnp.concatenate([query_grad, key_grad, value_grad], -1).astype(jnp.bfloat16)
    projector_grad = outer_sum(attn_in, qkv_grad)
    qkv_sums = jnp.sum(qkv_grad.astype(jnp.float32), (0, 1))
    projector_bias_grad = jnp.concatenate([qkv_sums[:model_width], qkv_sums[2 * model_width :]])
    attn_in_grad = matmul_back(qkv_grad, back_projector)
    scale_attn_grad = jnp.sum(attn_in_grad * normed_one, 1)
    shift_attn_grad = jnp.sum(attn_in_grad, 1)
    features_grad = hidden_grad + normalize_back(
        attn_in_grad * (1.0 + scale_attn), normed_one, inverse_one
    )
    partial_mod = jnp.concatenate(
        [
            shift_attn_grad,
            scale_attn_grad,
            gate_attn_grad,
            shift_mlp_grad,
            scale_mlp_grad,
            gate_mlp_grad,
        ],
        -1,
    )
    modulation_grad = lax.psum(partial_mod, "seq").astype(jnp.bfloat16)
    silu_grad = jnp.einsum(
        "le,de->ld", modulation_grad, back_modulator, preferred_element_type=jnp.float32
    )
    unused_silu, silu_back = jax.vjp(jax.nn.silu, cond_float)
    condition_grad = silu_back(silu_grad)[0]
    leader = (lax.axis_index("seq") == 0).astype(jnp.float32)
    modulator_grad = (
        jnp.einsum("ld,le->de", silu_low, modulation_grad, preferred_element_type=jnp.float32)
        * leader
    )
    modulator_bias_grad = jnp.sum(modulation_grad.astype(jnp.float32), 0) * leader
    summed = (
        lax.psum_scatter(
            modulator_grad.astype(jnp.bfloat16), "group", scatter_dimension=0, tiled=True
        ).astype(jnp.float32),
        lax.psum_scatter(
            modulator_bias_grad.astype(jnp.bfloat16), "group", scatter_dimension=0, tiled=True
        ).astype(jnp.float32),
        lax.psum_scatter(
            projector_grad.astype(jnp.bfloat16), "group", scatter_dimension=0, tiled=True
        ).astype(jnp.float32),
        lax.psum_scatter(
            projector_bias_grad.astype(jnp.bfloat16), "group", scatter_dimension=0, tiled=True
        ).astype(jnp.float32),
        lax.psum_scatter(
            combiner_grad.astype(jnp.bfloat16), "group", scatter_dimension=0, tiled=True
        ).astype(jnp.float32),
        lax.psum_scatter(
            combiner_bias_grad.astype(jnp.bfloat16), "group", scatter_dimension=0, tiled=True
        ).astype(jnp.float32),
        lax.psum_scatter(
            expander_grad.astype(jnp.bfloat16), "group", scatter_dimension=0, tiled=True
        ).astype(jnp.float32),
        lax.psum_scatter(
            expander_bias_grad.astype(jnp.bfloat16), "group", scatter_dimension=0, tiled=True
        ).astype(jnp.float32),
        lax.psum_scatter(
            reducer_grad.astype(jnp.bfloat16), "group", scatter_dimension=0, tiled=True
        ).astype(jnp.float32),
        lax.psum_scatter(
            reducer_bias_grad.astype(jnp.bfloat16), "group", scatter_dimension=0, tiled=True
        ).astype(jnp.float32),
    )
    totals = (
        lax.psum(summed[0].astype(jnp.bfloat16), ("replica", "seq")).astype(jnp.float32),
        lax.psum(summed[1].astype(jnp.bfloat16), ("replica", "seq")).astype(jnp.float32),
        lax.psum(summed[2].astype(jnp.bfloat16), ("replica", "seq")).astype(jnp.float32),
        lax.psum(summed[3].astype(jnp.bfloat16), ("replica", "seq")).astype(jnp.float32),
        lax.psum(summed[4].astype(jnp.bfloat16), ("replica", "seq")).astype(jnp.float32),
        lax.psum(summed[5].astype(jnp.bfloat16), ("replica", "seq")).astype(jnp.float32),
        lax.psum(summed[6].astype(jnp.bfloat16), ("replica", "seq")).astype(jnp.float32),
        lax.psum(summed[7].astype(jnp.bfloat16), ("replica", "seq")).astype(jnp.float32),
        lax.psum(summed[8].astype(jnp.bfloat16), ("replica", "seq")).astype(jnp.float32),
        lax.psum(summed[9].astype(jnp.bfloat16), ("replica", "seq")).astype(jnp.float32),
    )
    return (
        block_output,
        features_grad,
        condition_grad,
        totals[0],
        totals[1],
        totals[2],
        totals[3],
        totals[4],
        totals[5],
        totals[6],
        totals[7],
        totals[8],
        totals[9],
    )


def solution(mesh):
    return jax.shard_map(
        body,
        mesh=mesh,
        in_specs=(
            P(("group", "replica"), "seq", None),
            P(("group", "replica"), None),
            P("group", None),
            P("group"),
            P("group", None),
            P("group"),
            P("group", None),
            P("group"),
            P("group", None),
            P("group"),
            P("group", None),
            P("group"),
            P(("group", "replica"), "seq", None),
        ),
        out_specs=(
            P(("group", "replica"), "seq", None),
            P(("group", "replica"), "seq", None),
            P(("group", "replica"), None),
            P("group", None),
            P("group"),
            P("group", None),
            P("group"),
            P("group", None),
            P("group"),
            P("group", None),
            P("group"),
            P("group", None),
            P("group"),
        ),
        check_vma=False,
    )
```

profile of v0, /device:TPU:0, one launch (start us, length us, event | category | flops | bytes accessed | tf_op | source)
XLA Modules:
  0.0 2555.5 jit_solution(12768275986361563143)
XLA Ops:
  19.9 181.6 %all-gather.11.cloned.1.call-done = bf16[1152,6912]{1,0:T(8,128)(2,1)} async-done(((bf16[576,6912]{1,0:T(8,128)(2,1)}), bf16[1152,6912]{1,0:T(8,128)(2,1)}) %all-gather.11.cloned.1.call-update) | async-done | bytes 15925264 | tf_op jit(solution)/shard_map/all_gather | solution.py:153
  209.9 92.4 %all-gather.13.cloned.1.call-done = bf16[1152,3456]{1,0:T(8,128)(2,1)} async-done(((bf16[576,3456]{1,0:T(8,128)(2,1)}), bf16[1152,3456]{1,0:T(8,128)(2,1)}) %all-gather.13.cloned.1.call-update) | async-done | bytes 7962640 | tf_op jit(solution)/shard_map/all_gather | solution.py:155
  337.2 45.4 %all-gather.17.cloned.1.call-done = bf16[2,2048,1152]{2,1,0:T(8,128)(2,1)} async-done(((bf16[2,512,1152]{2,1,0:T(8,128)(2,1)}), bf16[2,2048,1152]{2,1,0:T(8,128)(2,1)}) %all-gather.17.cloned.1.call-update) | async-done | bytes 9437200 | tf_op jit(solution)/shard_map/all_gather | solution.py:200
  382.6 12.9 copy.64
  395.4 53.4 %all-gather.15.cloned.1.call-done = bf16[2,2048,1152]{2,1,0:T(8,128)(2,1)} async-done(((bf16[2,512,1152]{2,1,0:T(8,128)(2,1)}), bf16[2,2048,1152]{2,1,0:T(8,128)(2,1)}) %all-gather.15.cloned.1.call-update) | async-done | bytes 9437200 | tf_op jit(solution)/shard_map/all_gather | solution.py:199
  448.8 12.8 copy.63
  461.6 132.3 %while.53 = (s32[]{:T(128)}, bf16[2,512,1152]{1,2,0:T(8,128)(2,1)}, f32[2,16,512]{2,1,0:T(8,128)}, bf16[2,512,16,72]{1,3,2,0:T(8,128)(2,1)S(1)}, bf16[2,2048,16,...) while((s32[]{:T(128)}, bf16[2,512,1152]{1,2,0:T(8,128)(2,1)}, ...), condition=%wide.region_7.8_spmd, body=%wide.region_2.7_spmd.sunk | while | flops 1245706240 | bytes 105679224 | solution.py:202
  471.9 52.3 %while.56 = (s32[]{:T(128)}, bf16[4,512,4,72]{1,3,2,0:T(8,128)(2,1)}, f32[4,4,512]{2,1,0:T(4,128)}, bf16[4,2048,4,72]{1,3,2,0:T(8,128)(2,1)}, bf16[4,512,4,72]{1...) while((s32[]{:T(128)}, bf16[4,512,4,72]{1,3,2,0:T(8,128)(2,1)}, ...), condition=%wide.region_6.6_spmd, body=%wide.region_3.5_spmd.sunk | while | flops 1245706240 | bytes 63080592 | solution.py:73
  538.2 51.9 %while.56 = (s32[]{:T(128)}, bf16[4,512,4,72]{1,3,2,0:T(8,128)(2,1)}, f32[4,4,512]{2,1,0:T(4,128)}, bf16[4,2048,4,72]{1,3,2,0:T(8,128)(2,1)}, bf16[4,512,4,72]{1...) while((s32[]{:T(128)}, bf16[4,512,4,72]{1,3,2,0:T(8,128)(2,1)}, ...), condition=%wide.region_6.6_spmd, body=%wide.region_3.5_spmd.sunk | while | flops 1245706240 | bytes 63080592 | solution.py:73
  606.9 15.1 all-gather.21.cloned.1.call-done
  622.1 21.5 fusion.66
  643.5 111.0 %all-gather.23.cloned.1.call-done = bf16[4608,1152]{1,0:T(8,128)(2,1)} async-done(((bf16[2304,1152]{1,0:T(8,128)(2,1)}), bf16[4608,1152]{1,0:T(8,128)(2,1)}) %all-gather.23.cloned.1.call-update) | async-done | bytes 10616848 | tf_op jit(solution)/shard_map/all_gather | solution.py:161
  754.6 27.7 %fusion.122 = (bf16[4608]{0:T(1024)(128)(2,1)}, bf16[2,512,4608]{2,1,0:T(8,128)(2,1)S(1)}) fusion(f32[2,512,4608]{2,1,0:T(8,128)} %fusion.66, f32[4608]{0:T(1024)S(1)} %copy-done.32, bf16[4608,1152]{1,0:T(8,128)(2,1)} %all-gather.23.cloned.1.call-done, bf16[2,512,1152]{2,1,0:T(8,128)(2,1)S(1)} %copy-done.14, f32[2,1152]{1,0:T(2,128)S(1)} %copy-done.26), kind=kOutput, calls=%fused_computation.185 | convolution fusion | flops 10978979840 | bytes 41324544 | tf_op jit(solution)/shard_map/bte,de->btd/dot_general | solution.py:32
  786.0 17.7 fusion.64
  803.7 26.0 %fusion.90 = (f32[2,1152]{1,0:T(2,128)}, bf16[2,512,1152]{2,1,0:T(8,128)(2,1)}, f32[2,1152]{1,0:T(2,128)}, f32[2,512]{1,0:T(2,128)S(1)}, f32[2,512]{1,0:T(2,128)S(1)}, /*index=5*/f32[2,1152]{1,0:T(2,128)}) fusion(bf16[2,512,1152]{2,1,0:T(8,128)(2,1)S(1)} %copy-done.14, f32[2,512,1152]{2,1,0:T(8,128)} %copy-done.10, f32[2,1152]{1,0:T(2,128)S(1)} %copy-done.26, ...), kind=kOutput, calls=%fused_computation.123 | convolution fusion | flops 10937688064 | bytes 43732480 | tf_op jit(solution)/shard_map/btd,de->bte/dot_general | solution.py:28
  845.2 400.5 %while.55 = (s32[]{:T(128)}, bf16[2,512,1152]{2,1,0:T(8,128)(2,1)}, f32[2,2048,1152]{2,1,0:T(8,128)}, f32[2,2048,1152]{2,1,0:T(8,128)}, bf16[2,512,16,72]{1,3,2,...) while((s32[]{:T(128)}, bf16[2,512,1152]{2,1,0:T(8,128)(2,1)}, ...), condition=%wide.region_16.17_spmd, body=%wide.region_12.16_spmd.sunk | while | flops 3070965760 | bytes 315880896 | solution.py:256
  858.2 152.7 %while.57 = (s32[]{:T(128)}, bf16[4,512,4,72]{1,3,2,0:T(8,128)(2,1)}, f32[4,2048,4,72]{1,3,2,0:T(8,128)}, f32[4,2048,4,72]{1,3,2,0:T(8,128)}, bf16[4,2048,4,72]{...) while((s32[]{:T(128)}, ...), condition=%wide.region_15.15_spmd, body=%wide.region_13.14_spmd.sunk | while | flops 3070965760 | bytes 169473184 | solution.py:112
  1032.1 13.3 constant_dynamic-update-slice_fusion.18
  1058.2 152.7 %while.57 = (s32[]{:T(128)}, bf16[4,512,4,72]{1,3,2,0:T(8,128)(2,1)}, f32[4,2048,4,72]{1,3,2,0:T(8,128)}, f32[4,2048,4,72]{1,3,2,0:T(8,128)}, bf16[4,2048,4,72]{...) while((s32[]{:T(128)}, ...), condition=%wide.region_15.15_spmd, body=%wide.region_13.14_spmd.sunk | while | flops 3070965760 | bytes 169473184 | solution.py:112
  1232.2 13.3 constant_dynamic-update-slice_fusion.18
  1253.9 25.8 %fusion.52 = bf16[4608,1152]{1,0:T(8,128)(2,1)} fusion(bf16[2,512,1152]{2,1,0:T(8,128)(2,1)S(1)} %copy-done.15, f32[2,1152]{1,0:T(2,128)S(1)} %copy-done.27, f32[2,512,4608]{2,1,0:T(8,128)} %fusion.66, f32[4608]{0:T(1024)S(1)} %copy-done.33), kind=kOutput, calls=%fused_computation.75 | convolution fusion | flops 10927669248 | bytes 31878144 | tf_op jit(solution)/shard_map/btd,bte->de/dot_general | solution.py:36
  1280.5 18.6 fusion.51
  1299.1 84.6 %reduce-scatter.10.cloned.1.call-done = f32[2,512,1152]{2,1,0:T(8,128)} async-done(((f32[2,2048,1152]{2,1,0:T(8,128)}), f32[2,512,1152]{2,1,0:T(8,128)}) %reduce-scatter.10.cloned.1.call-update) | async-done | bytes 4718608 | tf_op jit(solution)/shard_map/reduce_scatter | solution.py:268
  1387.8 136.4 %reduce-scatter.8.cloned.1.call-done = f32[2,512,1152]{2,1,0:T(8,128)} async-done(((f32[2,2048,1152]{2,1,0:T(8,128)}), f32[2,512,1152]{2,1,0:T(8,128)}) %reduce-scatter.8.cloned.1.call-update) | async-done | bytes 4718608 | tf_op jit(solution)/shard_map/reduce_scatter | solution.py:267
  1528.4 12.7 fusion.60
  1541.4 16.0 fusion.87
  1584.2 107.0 %reduce-scatter.20.cloned.1.call-done = bf16[2304,1152]{1,0:T(8,128)(2,1)} async-done(((bf16[4608,1152]{1,0:T(8,128)(2,1)}), bf16[2304,1152]{1,0:T(8,128)(2,1)}) %reduce-scatter.20.cloned.1.call-update) | async-done | bytes 5308432 | tf_op jit(solution)/shard_map/reduce_scatter | solution.py:328
  1691.2 126.1 %reduce-scatter.18.cloned.1.call-done = bf16[576,4608]{1,0:T(8,128)(2,1)} async-done(((bf16[1152,4608]{1,0:T(8,128)(2,1)}), bf16[576,4608]{1,0:T(8,128)(2,1)}) %reduce-scatter.18.cloned.1.call-update) | async-done | bytes 5308432 | tf_op jit(solution)/shard_map/reduce_scatter | solution.py:322
  1817.3 97.7 %reduce-scatter.14.cloned.1.call-done = bf16[576,3456]{1,0:T(8,128)(2,1)} async-done(((bf16[1152,3456]{1,0:T(8,128)(2,1)}), bf16[576,3456]{1,0:T(8,128)(2,1)}) %reduce-scatter.14.cloned.1.call-update) | async-done | bytes 3981328 | tf_op jit(solution)/shard_map/reduce_scatter | solution.py:310
  1915.0 182.8 %reduce-scatter.12.cloned.1.call-done = bf16[576,6912]{1,0:T(8,128)(2,1)} async-done(((bf16[1152,6912]{1,0:T(8,128)(2,1)}), bf16[576,6912]{1,0:T(8,128)(2,1)}) %reduce-scatter.12.cloned.1.call-update) | async-done | bytes 7962640 | tf_op jit(solution)/shard_map/reduce_scatter | solution.py:304
  2112.0 63.2 %all-reduce.7 = (bf16[3456]{0:T(1024)(128)(2,1)S(1)}, bf16[1152]{0:T(1024)(128)(2,1)S(1)}, bf16[576]{0:T(1024)(128)(2,1)S(1)}, bf16[2304]{0:T(1024)(128)(2,1)S(1)}, bf16[576]{0:T(1024)(128)(2,1)S(1)}) all-reduce(bf16[3456]{0:T(1024)(128)(2,1)S(1)} %dynamic-slice.3, ...), channel_id=1, replica_groups=mesh['group'=2,'replica'=4,'seq'=4] {'replica','seq'}, use_global_device_ids=true, to_apply=%region_32.33 | all-reduce | flops 8064 | bytes 32256 | tf_op jit(solution)/shard_map/psum | solution.py:337
  2188.9 329.8 %all-reduce.13.cloned.1.call-done = (bf16[576,6912]{1,0:T(8,128)(2,1)}, bf16[576,3456]{1,0:T(8,128)(2,1)}, bf16[576,1152]{1,0:T(8,128)(2,1)}, bf16[576,4608]{1,0:T(8,128)(2,1)}, bf16[2304,1152]{1,0:T(8,128)(2,1)}) async-done(((bf16[576,6912]{1,0:T(8,128)(2,1)}, bf16[576,3456]{1,0:T(8,128)(2,1)}, bf16[576,1152]{1,0:T(8,128)(2,1)}, bf16[576,4608]{1,0:T(8,128)(2,1)}, bf16[2304,1152]{1,0:T(8,128)(2,1)}), ...) | async-done | bytes 23887888 | tf_op jit(solution)/shard_map/psum | solution.py:336
  (414 shorter events, 691.7 us)
Async XLA Ops:
  7.2 194.4 %all-gather.11.cloned.1.call-start = ((), (), s32[]{:S(2)}) async-start(), calls=%async_computation.7 | async-start | bytes 23887872 | tf_op jit(solution)/shard_map/all_gather | solution.py:153
  7.9 193.6 %copy-start.18 = (bf16[2,1152]{1,0:T(2,128)(2,1)S(1)}, bf16[2,1152]{1,0:T(2,128)(2,1)}, u32[]{:S(2)}) copy-start(bf16[2,1152]{1,0:T(2,128)(2,1)} %param.22) | copy-start | bytes 13828
  8.0 294.4 %all-gather.13.cloned.1.call-start = ((), (), s32[]{:S(2)}) async-start(), calls=%async_computation.8 | async-start | bytes 11943936 | tf_op jit(solution)/shard_map/all_gather | solution.py:155
  8.7 373.9 %all-gather.17.cloned.1.call-start = ((), (), s32[]{:S(2)}) async-start(), calls=%async_computation.10 | async-start | bytes 11796480 | tf_op jit(solution)/shard_map/all_gather | solution.py:200
  19.1 283.2 %copy-start.30 = (f32[2,512]{1,0:T(2,128)}, f32[2,512]{1,0:T(2,128)S(1)}, u32[]{:S(2)}) copy-start(f32[2,512]{1,0:T(2,128)S(1)} %broadcast_multiply_fusion.5) | copy-start | bytes 12292
  19.9 282.4 %copy-start.38 = (f32[2,512]{1,0:T(2,128)}, f32[2,512]{1,0:T(2,128)S(1)}, u32[]{:S(2)}) copy-start(f32[2,512]{1,0:T(2,128)S(1)} %add_rsqrt_fusion.1) | copy-start | bytes 12292
  209.9 105.1 %copy-start.22 = (f32[2,1152]{1,0:T(2,128)}, f32[2,1152]{1,0:T(2,128)S(1)}, u32[]{:S(2)}) copy-start(f32[2,1152]{1,0:T(2,128)S(1)} %get-tuple-element.313) | copy-start | bytes 27652
  209.9 105.1 %copy-start.41 = (f32[2,1152]{1,0:T(2,128)}, f32[2,1152]{1,0:T(2,128)S(1)}, u32[]{:S(2)}) copy-start(f32[2,1152]{1,0:T(2,128)S(1)} %get-tuple-element.312) | copy-start | bytes 27652
  318.2 130.6 %all-gather.15.cloned.1.call-start = ((), (), s32[]{:S(2)}) async-start(), calls=%async_computation.9 | async-start | bytes 11796480 | tf_op jit(solution)/shard_map/all_gather | solution.py:199
  318.8 275.1 %all-gather.19.cloned.1.call-start = ((), (), s32[]{:S(2)}) async-start(), calls=%async_computation.11 | async-start | bytes 3981312 | tf_op jit(solution)/shard_map/all_gather | solution.py:157
  319.4 302.6 %all-gather.21.cloned.1.call-start = ((), (), s32[]{:S(2)}) async-start(), calls=%async_computation.12 | async-start | bytes 15925248 | tf_op jit(solution)/shard_map/all_gather | solution.py:159
  320.0 434.5 %all-gather.23.cloned.1.call-start = ((), (), s32[]{:S(2)}) async-start(), calls=%async_computation.13 | async-start | bytes 15925248 | tf_op jit(solution)/shard_map/all_gather | solution.py:161
  320.7 1063.0 %reduce-scatter.10.cloned.1.call-start = ((), (), s32[]{:S(2)}) async-start(), calls=%async_computation.15 | async-start | bytes 23592960 | tf_op jit(solution)/shard_map/reduce_scatter | solution.py:268
  461.6 132.3 %copy-start.28 = (f32[2,1152]{1,0:T(2,128)S(1)}, f32[2,1152]{1,0:T(2,128)}, u32[]{:S(2)}) copy-start(f32[2,1152]{1,0:T(2,128)} %get-tuple-element.314) | copy-start | bytes 27652
  471.9 56.0 %copy-start.3 = (bf16[2,512,16,72]{1,3,2,0:T(8,128)(2,1)S(1)}, bf16[2,512,16,72]{1,3,2,0:T(8,128)(2,1)}, u32[]{:S(2)}) copy-start(bf16[2,512,16,72]{1,3,2,0:T(8,128)(2,1)} %copy-done.2) | copy-start | bytes 7077892 | tf_op jit(solution)/shard_map/while
  604.1 225.5 %copy-start.20 = (f32[2,512]{1,0:T(2,128)}, f32[2,512]{1,0:T(2,128)S(1)}, u32[]{:S(2)}) copy-start(f32[2,512]{1,0:T(2,128)S(1)} %broadcast_multiply_fusion.4) | copy-start | bytes 12292
  606.9 222.8 %copy-start.36 = (f32[2,512]{1,0:T(2,128)}, f32[2,512]{1,0:T(2,128)S(1)}, u32[]{:S(2)}) copy-start(f32[2,512]{1,0:T(2,128)S(1)} %add_rsqrt_fusion) | copy-start | bytes 12292
  622.0 132.5 %copy-start.14 = (bf16[2,512,1152]{2,1,0:T(8,128)(2,1)S(1)}, bf16[2,512,1152]{2,1,0:T(8,128)(2,1)}, u32[]{:S(2)}) copy-start(bf16[2,512,1152]{2,1,0:T(8,128)(2,1)} %param.33) | copy-start | bytes 7077892
  622.0 132.5 %copy-start.26 = (f32[2,1152]{1,0:T(2,128)S(1)}, f32[2,1152]{1,0:T(2,128)}, u32[]{:S(2)}) copy-start(f32[2,1152]{1,0:T(2,128)} %get-tuple-element.309) | copy-start | bytes 27652
  622.0 132.5 %copy-start.32 = (f32[4608]{0:T(1024)S(1)}, f32[4608]{0:T(1024)}, u32[]{:S(2)}) copy-start(f32[4608]{0:T(1024)} %reshape.180) | copy-start | bytes 55300
  1245.8 278.4 %reduce-scatter.8.cloned.1.call-start = ((), (), s32[]{:S(2)}) async-start(), calls=%async_computation.14 | async-start | bytes 23592960 | tf_op jit(solution)/shard_map/reduce_scatter | solution.py:267
  1246.5 337.7 %reduce-scatter.16.cloned.1.call-start = ((), (), s32[]{:S(2)}) async-start(), calls=%async_computation.18 | async-start | bytes 3981312 | tf_op jit(solution)/shard_map/reduce_scatter | solution.py:316
  1253.9 437.3 %reduce-scatter.20.cloned.1.call-start = ((), (), s32[]{:S(2)}) async-start(), calls=%async_computation.20 | async-start | bytes 15925248 | tf_op jit(solution)/shard_map/reduce_scatter | solution.py:328
  1279.8 537.5 %reduce-scatter.18.cloned.1.call-start = ((), (), s32[]{:S(2)}) async-start(), calls=%async_computation.19 | async-start | bytes 15925248 | tf_op jit(solution)/shard_map/reduce_scatter | solution.py:322
  1299.1 615.9 %reduce-scatter.14.cloned.1.call-start = ((), (), s32[]{:S(2)}) async-start(), calls=%async_computation.17 | async-start | bytes 11943936 | tf_op jit(solution)/shard_map/reduce_scatter | solution.py:310
  1383.7 144.7 %copy-start.23 = (f32[2,1152]{1,0:T(2,128)S(1)}, f32[2,1152]{1,0:T(2,128)}, u32[]{:S(2)}) copy-start(f32[2,1152]{1,0:T(2,128)} %copy-done.22) | copy-start | bytes 27652
  1383.7 144.7 %copy-start.31 = (f32[2,512]{1,0:T(2,128)S(1)}, f32[2,512]{1,0:T(2,128)}, u32[]{:S(2)}) copy-start(f32[2,512]{1,0:T(2,128)} %copy-done.30) | copy-start | bytes 12292
  1383.7 144.7 %copy-start.39 = (f32[2,512]{1,0:T(2,128)S(1)}, f32[2,512]{1,0:T(2,128)}, u32[]{:S(2)}) copy-start(f32[2,512]{1,0:T(2,128)} %copy-done.38) | copy-start | bytes 12292
  1383.7 144.7 %copy-start.42 = (f32[2,1152]{1,0:T(2,128)S(1)}, f32[2,1152]{1,0:T(2,128)}, u32[]{:S(2)}) copy-start(f32[2,1152]{1,0:T(2,128)} %copy-done.41) | copy-start | bytes 27652
  1387.8 140.6 %copy-start.9 = (bf16[2,512,1152]{2,1,0:T(8,128)(2,1)S(1)}, bf16[2,512,1152]{2,1,0:T(8,128)(2,1)}, u32[]{:S(2)}) copy-start(bf16[2,512,1152]{2,1,0:T(8,128)(2,1)} %param.21) | copy-start | bytes 7077892
  1541.2 556.6 %reduce-scatter.12.cloned.1.call-start = ((), (), s32[]{:S(2)}) async-start(), calls=%async_computation.16 | async-start | bytes 23887872 | tf_op jit(solution)/shard_map/reduce_scatter | solution.py:304
  1584.2 934.5 %all-reduce.13.cloned.1.call-start = ((), (), s32[]{:S(2)}) async-start(), calls=%async_computation.21 | async-start | bytes 47775744 | tf_op jit(solution)/shard_map/psum | solution.py:336
  (69 other events, 497.2 us)
Sparse Core Ops, SparseCore 0:
  9.6 191.9 all-gather.10
  203.1 99.1 all-gather.12
  318.3 64.2 all-gather.16
  384.6 64.2 all-gather.14
  450.2 39.3 all-gather.18
  491.0 130.9 all-gather.20
  623.6 130.9 all-gather.22
  1245.9 137.8 reduce-scatter.9
  1386.3 137.8 reduce-scatter.7
  1526.9 38.0 reduce-scatter.15
  1567.8 123.3 reduce-scatter.19
  1693.9 123.3 reduce-scatter.17
  1820.2 94.7 reduce-scatter.13
  1917.7 180.0 reduce-scatter.11
  2102.9 415.7 all-reduce.12
where the time goes:
time: 2570 us; the launch traced here: 2560 us
  waiting for transfers between devices  1570 us (61%)
  matrix products  518 us (20%)
  other arithmetic  177 us (7%)
  local copies, waits for them, and re-layouts  172 us (7%)
  blocking collectives  100 us (4%)
    psum x1, waiting for transfers between devices, body(): lax.psum(summed[0].astype(jnp.bfloat16), ('replica', 'seq'))  330 us
    reduce_scatter x1, waiting for transfers between devices, body(): lax.psum_scatter(modulator_grad.astype(jnp.bfloat16), 'group', scatter_di...  183 us
    all_gather x1, waiting for transfers between devices, body(): lax.all_gather(shards[0], 'group', axis=0, tiled=True)  182 us
    reduce_scatter x1, waiting for transfers between devices, body(): lax.psum_scatter(key_part, 'seq', scatter_dimension=1, tiled=True)  136 us
    reduce_scatter x1, waiting for transfers between devices, body(): lax.psum_scatter(expander_grad.astype(jnp.bfloat16), 'group', scatter_dim...  126 us
    all_gather x1, waiting for transfers between devices, body(): lax.all_gather(shards[8], 'group', axis=0, tiled=True)  111 us
    reduce_scatter x1, waiting for transfers between devices, body(): lax.psum_scatter(reducer_grad.astype(jnp.bfloat16), 'group', scatter_dime...  107 us
    reduce_scatter x1, waiting for transfers between devices, body(): lax.psum_scatter(projector_grad.astype(jnp.bfloat16), 'group', scatter_di...  97.7 us
  transfers between devices with their start and end apart: 15, of which 13 were waited for; matrix products, arithmetic and copies ran while one was open for 13% of the time, Pallas kernels for 0%

commit v1 on v0

--- a/solution.py
+++ b/solution.py
@@ -333,7 +333,9 @@
         ).astype(jnp.float32),
     )
     totals = (
-        lax.psum(summed[0].astype(jnp.bfloat16), ("replica", "seq")).astype(jnp.float32),
+        jnp.sum(lax.all_gather(summed[0].astype(jnp.bfloat16), ("replica", "seq")), axis=0).astype(
+            jnp.float32
+        ),
         lax.psum(summed[1].astype(jnp.bfloat16), ("replica", "seq")).astype(jnp.float32),
         lax.psum(summed[2].astype(jnp.bfloat16), ("replica", "seq")).astype(jnp.float32),
         lax.psum(summed[3].astype(jnp.bfloat16), ("replica", "seq")).astype(jnp.float32),

time: 2570 us -> 3070 us (1.19)
  waiting for transfers between devices: 1570 us -> 2030 us
  other arithmetic: 177 us -> 222 us
    all_gather x0 -> x1, waiting for transfers between devices: none -> 590 us  [body(): lax.all_gather(summed[0].astype(jnp.bfloat16), ('replica', 'seq'))]
    psum x1, waiting for transfers between devices: 330 us -> 198 us  [body(): lax.psum(summed[2].astype(jnp.bfloat16), ('replica', 'seq'))]
    reduce_sum x0 -> x1, other arithmetic: none -> 43.4 us  [body(): jnp.sum(lax.all_gather(summed[0].astype(jnp.bfloat16), ('replica', 'seq')...]
  transfers between devices with their start and end apart: 15 -> 16, of which waited for: 13 -> 14; matrix products, arithmetic and copies ran while one was open for 13% -> 11% of each run, Pallas kernels for 0% -> 0%
where the time goes in v1:
time: 3070 us; the launch traced here: 3060 us
  waiting for transfers between devices  2030 us (66%)
  matrix products  518 us (17%)
  other arithmetic  222 us (7%)
  local copies, waits for them, and re-layouts  172 us (6%)
  blocking collectives  100 us (3%)
    all_gather x1, waiting for transfers between devices, body(): lax.all_gather(summed[0].astype(jnp.bfloat16), ('replica', 'seq'))  590 us
    psum x1, waiting for transfers between devices, body(): lax.psum(summed[2].astype(jnp.bfloat16), ('replica', 'seq'))  198 us
    reduce_scatter x1, waiting for transfers between devices, body(): lax.psum_scatter(modulator_grad.astype(jnp.bfloat16), 'group', scatter_di...  183 us
    all_gather x1, waiting for transfers between devices, body(): lax.all_gather(shards[0], 'group', axis=0, tiled=True)  182 us
    reduce_scatter x1, waiting for transfers between devices, body(): lax.psum_scatter(key_part, 'seq', scatter_dimension=1, tiled=True)  136 us
    reduce_scatter x1, waiting for transfers between devices, body(): lax.psum_scatter(expander_grad.astype(jnp.bfloat16), 'group', scatter_dim...  126 us
    all_gather x1, waiting for transfers between devices, body(): lax.all_gather(shards[8], 'group', axis=0, tiled=True)  111 us
    reduce_scatter x1, waiting for transfers between devices, body(): lax.psum_scatter(reducer_grad.astype(jnp.bfloat16), 'group', scatter_dime...  107 us
  transfers between devices with their start and end apart: 16, of which 14 were waited for; matrix products, arithmetic and copies ran while one was open for 11% of the time, Pallas kernels for 0%

profile of v1, /device:TPU:0, one launch (start us, length us, event | category | flops | bytes accessed | tf_op | source)
XLA Modules:
  0.0 3059.1 jit_solution(12396778991393922014)
XLA Ops:
  19.9 181.6 %all-gather.13.cloned.1.call-done = bf16[1152,6912]{1,0:T(8,128)(2,1)} async-done(((bf16[576,6912]{1,0:T(8,128)(2,1)}), bf16[1152,6912]{1,0:T(8,128)(2,1)}) %all-gather.13.cloned.1.call-update) | async-done | bytes 15925264 | tf_op jit(solution)/shard_map/all_gather | solution.py:153
  209.9 92.4 %all-gather.15.cloned.1.call-done = bf16[1152,3456]{1,0:T(8,128)(2,1)} async-done(((bf16[576,3456]{1,0:T(8,128)(2,1)}), bf16[1152,3456]{1,0:T(8,128)(2,1)}) %all-gather.15.cloned.1.call-update) | async-done | bytes 7962640 | tf_op jit(solution)/shard_map/all_gather | solution.py:155
  337.1 45.4 %all-gather.19.cloned.1.call-done = bf16[2,2048,1152]{2,1,0:T(8,128)(2,1)} async-done(((bf16[2,512,1152]{2,1,0:T(8,128)(2,1)}), bf16[2,2048,1152]{2,1,0:T(8,128)(2,1)}) %all-gather.19.cloned.1.call-update) | async-done | bytes 9437200 | tf_op jit(solution)/shard_map/all_gather | solution.py:200
  382.6 12.9 copy.64
  395.4 53.4 %all-gather.17.cloned.1.call-done = bf16[2,2048,1152]{2,1,0:T(8,128)(2,1)} async-done(((bf16[2,512,1152]{2,1,0:T(8,128)(2,1)}), bf16[2,2048,1152]{2,1,0:T(8,128)(2,1)}) %all-gather.17.cloned.1.call-update) | async-done | bytes 9437200 | tf_op jit(solution)/shard_map/all_gather | solution.py:199
  461.6 132.3 %while.53 = (s32[]{:T(128)}, bf16[2,512,1152]{1,2,0:T(8,128)(2,1)}, f32[2,16,512]{2,1,0:T(8,128)}, bf16[2,512,16,72]{1,3,2,0:T(8,128)(2,1)S(1)}, bf16[2,2048,16,...) while((s32[]{:T(128)}, bf16[2,512,1152]{1,2,0:T(8,128)(2,1)}, ...), condition=%wide.region_7.8_spmd, body=%wide.region_2.7_spmd.sunk | while | flops 1245706240 | bytes 105679224 | solution.py:202
  471.9 52.3 %while.56 = (s32[]{:T(128)}, bf16[4,512,4,72]{1,3,2,0:T(8,128)(2,1)}, f32[4,4,512]{2,1,0:T(4,128)}, bf16[4,2048,4,72]{1,3,2,0:T(8,128)(2,1)}, bf16[4,512,4,72]{1...) while((s32[]{:T(128)}, bf16[4,512,4,72]{1,3,2,0:T(8,128)(2,1)}, ...), condition=%wide.region_6.6_spmd, body=%wide.region_3.5_spmd.sunk | while | flops 1245706240 | bytes 63080592 | solution.py:73
  538.2 51.9 %while.56 = (s32[]{:T(128)}, bf16[4,512,4,72]{1,3,2,0:T(8,128)(2,1)}, f32[4,4,512]{2,1,0:T(4,128)}, bf16[4,2048,4,72]{1,3,2,0:T(8,128)(2,1)}, bf16[4,512,4,72]{1...) while((s32[]{:T(128)}, bf16[4,512,4,72]{1,3,2,0:T(8,128)(2,1)}, ...), condition=%wide.region_6.6_spmd, body=%wide.region_3.5_spmd.sunk | while | flops 1245706240 | bytes 63080592 | solution.py:73
  606.9 15.1 all-gather.23.cloned.1.call-done
  622.1 21.5 fusion.66
  643.5 111.0 %all-gather.25.cloned.1.call-done = bf16[4608,1152]{1,0:T(8,128)(2,1)} async-done(((bf16[2304,1152]{1,0:T(8,128)(2,1)}), bf16[4608,1152]{1,0:T(8,128)(2,1)}) %all-gather.25.cloned.1.call-update) | async-done | bytes 10616848 | tf_op jit(solution)/shard_map/all_gather | solution.py:161
  754.6 27.7 fusion.122
  786.0 17.7 fusion.64
  803.6 26.0 fusion.90
  845.1 401.0 %while.55 = (s32[]{:T(128)}, bf16[2,512,1152]{2,1,0:T(8,128)(2,1)}, f32[2,2048,1152]{2,1,0:T(8,128)}, f32[2,2048,1152]{2,1,0:T(8,128)}, bf16[2,512,16,72]{1,3,2,...) while((s32[]{:T(128)}, bf16[2,512,1152]{2,1,0:T(8,128)(2,1)}, ...), condition=%wide.region_16.17_spmd, body=%wide.region_12.16_spmd.sunk | while | flops 3070965760 | bytes 315880896 | solution.py:256
  858.1 153.1 %while.57 = (s32[]{:T(128)}, bf16[4,512,4,72]{1,3,2,0:T(8,128)(2,1)}, f32[4,2048,4,72]{1,3,2,0:T(8,128)}, f32[4,2048,4,72]{1,3,2,0:T(8,128)}, bf16[4,2048,4,72]{...) while((s32[]{:T(128)}, ...), condition=%wide.region_15.15_spmd, body=%wide.region_13.14_spmd.sunk | while | flops 3070965760 | bytes 169473184 | solution.py:112
  1032.3 13.2 constant_dynamic-update-slice_fusion.18
  1058.4 153.1 %while.57 = (s32[]{:T(128)}, bf16[4,512,4,72]{1,3,2,0:T(8,128)(2,1)}, f32[4,2048,4,72]{1,3,2,0:T(8,128)}, f32[4,2048,4,72]{1,3,2,0:T(8,128)}, bf16[4,2048,4,72]{...) while((s32[]{:T(128)}, ...), condition=%wide.region_15.15_spmd, body=%wide.region_13.14_spmd.sunk | while | flops 3070965760 | bytes 169473184 | solution.py:112
  1232.6 13.4 constant_dynamic-update-slice_fusion.18
  1254.3 25.8 fusion.52
  1280.9 18.6 fusion.51
  1299.5 84.6 %reduce-scatter.10.cloned.1.call-done = f32[2,512,1152]{2,1,0:T(8,128)} async-done(((f32[2,2048,1152]{2,1,0:T(8,128)}), f32[2,512,1152]{2,1,0:T(8,128)}) %reduce-scatter.10.cloned.1.call-update) | async-done | bytes 4718608 | tf_op jit(solution)/shard_map/reduce_scatter | solution.py:268
  1388.2 136.4 %reduce-scatter.8.cloned.1.call-done = f32[2,512,1152]{2,1,0:T(8,128)} async-done(((f32[2,2048,1152]{2,1,0:T(8,128)}), f32[2,512,1152]{2,1,0:T(8,128)}) %reduce-scatter.8.cloned.1.call-update) | async-done | bytes 4718608 | tf_op jit(solution)/shard_map/reduce_scatter | solution.py:267
  1541.7 16.0 fusion.87
  1584.5 107.0 %reduce-scatter.20.cloned.1.call-done = bf16[2304,1152]{1,0:T(8,128)(2,1)} async-done(((bf16[4608,1152]{1,0:T(8,128)(2,1)}), bf16[2304,1152]{1,0:T(8,128)(2,1)}) %reduce-scatter.20.cloned.1.call-update) | async-done | bytes 5308432 | tf_op jit(solution)/shard_map/reduce_scatter | solution.py:328
  1691.6 126.1 %reduce-scatter.18.cloned.1.call-done = bf16[576,4608]{1,0:T(8,128)(2,1)} async-done(((bf16[1152,4608]{1,0:T(8,128)(2,1)}), bf16[576,4608]{1,0:T(8,128)(2,1)}) %reduce-scatter.18.cloned.1.call-update) | async-done | bytes 5308432 | tf_op jit(solution)/shard_map/reduce_scatter | solution.py:322
  1817.7 97.7 %reduce-scatter.14.cloned.1.call-done = bf16[576,3456]{1,0:T(8,128)(2,1)} async-done(((bf16[1152,3456]{1,0:T(8,128)(2,1)}), bf16[576,3456]{1,0:T(8,128)(2,1)}) %reduce-scatter.14.cloned.1.call-update) | async-done | bytes 3981328 | tf_op jit(solution)/shard_map/reduce_scatter | solution.py:310
  1915.5 182.7 %reduce-scatter.12.cloned.1.call-done = bf16[576,6912]{1,0:T(8,128)(2,1)} async-done(((bf16[1152,6912]{1,0:T(8,128)(2,1)}), bf16[576,6912]{1,0:T(8,128)(2,1)}) %reduce-scatter.12.cloned.1.call-update) | async-done | bytes 7962640 | tf_op jit(solution)/shard_map/reduce_scatter | solution.py:304
  2112.0 63.2 %all-reduce.7 = (bf16[3456]{0:T(1024)(128)(2,1)S(1)}, bf16[1152]{0:T(1024)(128)(2,1)S(1)}, bf16[576]{0:T(1024)(128)(2,1)S(1)}, bf16[2304]{0:T(1024)(128)(2,1)S(1)}, bf16[576]{0:T(1024)(128)(2,1)S(1)}) all-reduce(bf16[3456]{0:T(1024)(128)(2,1)S(1)} %dynamic-slice.3, ...), channel_id=1, replica_groups=mesh['group'=2,'replica'=4,'seq'=4] {'replica','seq'}, use_global_device_ids=true, to_apply=%region_32.33 | all-reduce | flops 8064 | bytes 32256 | tf_op jit(solution)/shard_map/psum | solution.py:339
  2188.8 198.2 %all-reduce.13.cloned.1.call-done = (bf16[576,3456]{1,0:T(8,128)(2,1)}, bf16[576,1152]{1,0:T(8,128)(2,1)}, bf16[576,4608]{1,0:T(8,128)(2,1)}, bf16[2304,1152]{1,0:T(8,128)(2,1)}) async-done(((bf16[576,3456]{1,0:T(8,128)(2,1)}, bf16[576,1152]{1,0:T(8,128)(2,1)}, bf16[576,4608]{1,0:T(8,128)(2,1)}, bf16[2304,1152]{1,0:T(8,128)(2,1)}), (bf16[576,3456]{1,0:T(8,128)(2,1)}, bf16[576,1152]{1,0:T(8,128)(2,1)}, ...) | async-done | bytes 15925264 | tf_op jit(solution)/shard_map/psum | solution.py:340
  2408.1 590.5 %all-gather.27.cloned.1.call-done = bf16[9216,6912]{1,0:T(8,128)(2,1)} async-done(((bf16[576,6912]{1,0:T(8,128)(2,1)}), bf16[9216,6912]{1,0:T(8,128)(2,1)}) %all-gather.27.cloned.1.call-update) | async-done | bytes 127402000 | tf_op jit(solution)/shard_map/all_gather | solution.py:336
  2998.6 43.4 %reduce_sum.224 = bf16[576,6912]{1,0:T(8,128)(2,1)} reduce(bf16[16,576,6912]{2,1,0:T(8,128)(2,1)} %bitcast.48, bf16[]{:T(256)} %constant.123.clone.1), dimensions={0}, to_apply=%region_29.30 | reduce | flops 59719680 | bytes 135364608 | tf_op jit(solution)/shard_map/reduce_sum | solution.py:336
  (420 shorter events, 718.9 us)
Async XLA Ops:
  7.2 194.4 %all-gather.13.cloned.1.call-start = ((), (), s32[]{:S(2)}) async-start(), calls=%async_computation.7 | async-start | bytes 23887872 | tf_op jit(solution)/shard_map/all_gather | solution.py:153
  7.9 193.6 %copy-start.19 = (bf16[2,1152]{1,0:T(2,128)(2,1)S(1)}, bf16[2,1152]{1,0:T(2,128)(2,1)}, u32[]{:S(2)}) copy-start(bf16[2,1152]{1,0:T(2,128)(2,1)} %param.22) | copy-start | bytes 13828
  8.0 294.4 %all-gather.15.cloned.1.call-start = ((), (), s32[]{:S(2)}) async-start(), calls=%async_computation.8 | async-start | bytes 11943936 | tf_op jit(solution)/shard_map/all_gather | solution.py:155
  8.7 373.9 %all-gather.19.cloned.1.call-start = ((), (), s32[]{:S(2)}) async-start(), calls=%async_computation.10 | async-start | bytes 11796480 | tf_op jit(solution)/shard_map/all_gather | solution.py:200
  19.1 283.2 %copy-start.31 = (f32[2,512]{1,0:T(2,128)}, f32[2,512]{1,0:T(2,128)S(1)}, u32[]{:S(2)}) copy-start(f32[2,512]{1,0:T(2,128)S(1)} %broadcast_multiply_fusion.5) | copy-start | bytes 12292
  19.9 282.4 %copy-start.39 = (f32[2,512]{1,0:T(2,128)}, f32[2,512]{1,0:T(2,128)S(1)}, u32[]{:S(2)}) copy-start(f32[2,512]{1,0:T(2,128)S(1)} %add_rsqrt_fusion.1) | copy-start | bytes 12292
  209.9 105.1 %copy-start.42 = (f32[2,1152]{1,0:T(2,128)}, f32[2,1152]{1,0:T(2,128)S(1)}, u32[]{:S(2)}) copy-start(f32[2,1152]{1,0:T(2,128)S(1)} %get-tuple-element.311) | copy-start | bytes 27652
  318.2 130.6 %all-gather.17.cloned.1.call-start = ((), (), s32[]{:S(2)}) async-start(), calls=%async_computation.9 | async-start | bytes 11796480 | tf_op jit(solution)/shard_map/all_gather | solution.py:199
  318.8 275.1 %all-gather.21.cloned.1.call-start = ((), (), s32[]{:S(2)}) async-start(), calls=%async_computation.11 | async-start | bytes 3981312 | tf_op jit(solution)/shard_map/all_gather | solution.py:157
  319.4 302.6 %all-gather.23.cloned.1.call-start = ((), (), s32[]{:S(2)}) async-start(), calls=%async_computation.12 | async-start | bytes 15925248 | tf_op jit(solution)/shard_map/all_gather | solution.py:159
  320.0 434.5 %all-gather.25.cloned.1.call-start = ((), (), s32[]{:S(2)}) async-start(), calls=%async_computation.13 | async-start | bytes 15925248 | tf_op jit(solution)/shard_map/all_gather | solution.py:161
  320.7 1063.4 %reduce-scatter.10.cloned.1.call-start = ((), (), s32[]{:S(2)}) async-start(), calls=%async_computation.15 | async-start | bytes 23592960 | tf_op jit(solution)/shard_map/reduce_scatter | solution.py:268
  461.6 132.3 %copy-start.29 = (f32[2,1152]{1,0:T(2,128)S(1)}, f32[2,1152]{1,0:T(2,128)}, u32[]{:S(2)}) copy-start(f32[2,1152]{1,0:T(2,128)} %get-tuple-element.313) | copy-start | bytes 27652
  604.1 225.5 %copy-start.21 = (f32[2,512]{1,0:T(2,128)}, f32[2,512]{1,0:T(2,128)S(1)}, u32[]{:S(2)}) copy-start(f32[2,512]{1,0:T(2,128)S(1)} %broadcast_multiply_fusion.4) | copy-start | bytes 12292
  606.9 222.7 %copy-start.37 = (f32[2,512]{1,0:T(2,128)}, f32[2,512]{1,0:T(2,128)S(1)}, u32[]{:S(2)}) copy-start(f32[2,512]{1,0:T(2,128)S(1)} %add_rsqrt_fusion) | copy-start | bytes 12292
  622.0 132.5 %copy-start.15 = (bf16[2,512,1152]{2,1,0:T(8,128)(2,1)S(1)}, bf16[2,512,1152]{2,1,0:T(8,128)(2,1)}, u32[]{:S(2)}) copy-start(bf16[2,512,1152]{2,1,0:T(8,128)(2,1)} %param.33) | copy-start | bytes 7077892
  622.0 132.5 %copy-start.27 = (f32[2,1152]{1,0:T(2,128)S(1)}, f32[2,1152]{1,0:T(2,128)}, u32[]{:S(2)}) copy-start(f32[2,1152]{1,0:T(2,128)} %get-tuple-element.308) | copy-start | bytes 27652
  622.0 132.5 %copy-start.33 = (f32[4608]{0:T(1024)S(1)}, f32[4608]{0:T(1024)}, u32[]{:S(2)}) copy-start(f32[4608]{0:T(1024)} %reshape.181) | copy-start | bytes 55300
  1246.2 278.4 %reduce-scatter.8.cloned.1.call-start = ((), (), s32[]{:S(2)}) async-start(), calls=%async_computation.14 | async-start | bytes 23592960 | tf_op jit(solution)/shard_map/reduce_scatter | solution.py:267
  1246.9 337.6 %reduce-scatter.16.cloned.1.call-start = ((), (), s32[]{:S(2)}) async-start(), calls=%async_computation.18 | async-start | bytes 3981312 | tf_op jit(solution)/shard_map/reduce_scatter | solution.py:316
  1254.3 437.3 %reduce-scatter.20.cloned.1.call-start = ((), (), s32[]{:S(2)}) async-start(), calls=%async_computation.20 | async-start | bytes 15925248 | tf_op jit(solution)/shard_map/reduce_scatter | solution.py:328
  1280.2 537.5 %reduce-scatter.18.cloned.1.call-start = ((), (), s32[]{:S(2)}) async-start(), calls=%async_computation.19 | async-start | bytes 15925248 | tf_op jit(solution)/shard_map/reduce_scatter | solution.py:322
  1299.5 615.9 %reduce-scatter.14.cloned.1.call-start = ((), (), s32[]{:S(2)}) async-start(), calls=%async_computation.17 | async-start | bytes 11943936 | tf_op jit(solution)/shard_map/reduce_scatter | solution.py:310
  1384.1 144.6 %copy-start.24 = (f32[2,1152]{1,0:T(2,128)S(1)}, f32[2,1152]{1,0:T(2,128)}, u32[]{:S(2)}) copy-start(f32[2,1152]{1,0:T(2,128)} %copy-done.23) | copy-start | bytes 27652
  1384.1 144.6 %copy-start.32 = (f32[2,512]{1,0:T(2,128)S(1)}, f32[2,512]{1,0:T(2,128)}, u32[]{:S(2)}) copy-start(f32[2,512]{1,0:T(2,128)} %copy-done.31) | copy-start | bytes 12292
  1384.1 144.6 %copy-start.40 = (f32[2,512]{1,0:T(2,128)S(1)}, f32[2,512]{1,0:T(2,128)}, u32[]{:S(2)}) copy-start(f32[2,512]{1,0:T(2,128)} %copy-done.39) | copy-start | bytes 12292
  1384.1 144.6 %copy-start.43 = (f32[2,1152]{1,0:T(2,128)S(1)}, f32[2,1152]{1,0:T(2,128)}, u32[]{:S(2)}) copy-start(f32[2,1152]{1,0:T(2,128)} %copy-done.42) | copy-start | bytes 27652
  1388.2 140.6 %copy-start.9 = (bf16[2,512,1152]{2,1,0:T(8,128)(2,1)S(1)}, bf16[2,512,1152]{2,1,0:T(8,128)(2,1)}, u32[]{:S(2)}) copy-start(bf16[2,512,1152]{2,1,0:T(8,128)(2,1)} %param.21) | copy-start | bytes 7077892
  1541.5 556.7 %reduce-scatter.12.cloned.1.call-start = ((), (), s32[]{:S(2)}) async-start(), calls=%async_computation.16 | async-start | bytes 23887872 | tf_op jit(solution)/shard_map/reduce_scatter | solution.py:304
  1584.5 802.5 %all-reduce.13.cloned.1.call-start = ((), (), s32[]{:S(2)}) async-start(), calls=%async_computation.22 | async-start | bytes 31850496 | tf_op jit(solution)/shard_map/psum | solution.py:340
  1915.4 185.1 %copy-start.12 = (bf16[2,512,1152]{2,1,0:T(8,128)(2,1)S(1)}, bf16[2,512,1152]{2,1,0:T(8,128)(2,1)}, u32[]{:S(2)}) copy-start(bf16[2,512,1152]{2,1,0:T(8,128)(2,1)} %convert.21) | copy-start | bytes 7077892
  1915.4 1083.2 %all-gather.27.cloned.1.call-start = ((), (), s32[]{:S(2)}) async-start(), calls=%async_computation.21 | async-start | bytes 135364608 | tf_op jit(solution)/shard_map/all_gather | solution.py:336
  (71 other events, 637.6 us)
Sparse Core Ops, SparseCore 0:
  9.6 191.9 all-gather.12
  203.1 99.1 all-gather.14
  318.3 64.2 all-gather.18
  384.6 64.2 all-gather.16
  450.2 39.3 all-gather.20
  491.0 130.9 all-gather.22
  623.6 130.9 all-gather.24
  1246.3 137.8 reduce-scatter.9
  1386.7 137.8 reduce-scatter.7
  1527.3 38.0 reduce-scatter.15
  1568.2 123.3 reduce-scatter.19
  1694.3 123.3 reduce-scatter.17
  1820.6 94.7 reduce-scatter.13
  1918.1 180.0 reduce-scatter.11
  2102.6 284.3 all-reduce.12
  2388.4 610.1 all-gather.26
